TPU v7x, 128 devices: a whole 4x4x4 slice. The times are simulated.
128 devices in a mesh: row: 16 (over x, y_hi, core), col: 8 (over z, y_lo).
Axes of the slice: x: 4, y: 4 (y_hi: 2, y_lo: 2; y = y_hi * 2 + y_lo), z: 4, core: 2. Of those that a mesh axis runs over, the one named last changes fastest.
Arguments:
- a_vals: bfloat16 [512, 8, 64, 1024], P('row', 'col'), may hold values from -0.0625 to 0.0625
- a_cols: int32 [512, 8, 16], P('row', 'col'), may hold values from 0 to 63, all different within a row
- p_vals: bfloat16 [512, 64, 256], P(('row', 'col')), may hold values from -1.5 to 1.5
- p_cols: int32 [512, 4], P(('row', 'col')), may hold values from 0 to 15, all different within a row
Outputs:
- coarse_op: float32 [1024, 1024], P('row', 'col')
Inputs may be any that keep to these rules, and one draw needn't show every extreme that they name: `a_cols`: within one fine block row and column range the 16 entries are distinct. `p_cols`: within one fine block row the 4 entries are distinct.
All inputs are finite; a program needn't handle non-finite values.
Results may differ from a plain program's by a relative error of at most 0.0003.
Values may be sent and summed in bfloat16 or wider, within the bound.
No kernel may reach another device: no remote copies, remote signals or barrier semaphores. Data moves between devices by JAX's collectives and lax.ppermute only.
A program may use at most 128 MiB of HBM per device.

v0:
```python
import math
import jax
import jax.numpy as jnp
from jax import lax
from jax.sharding import PartitionSpec as P


def from_root(value, axis, source):
    kept = jnp.where(lax.axis_index(axis) == source, value, 0).astype(value.dtype)
    return lax.psum(kept, axis)


def contract_rows(p_slabs, p_kinds, wide, coarse):
    fine_rows = p_slabs.shape[0]
    block = p_slabs.shape[1]
    touched = p_kinds.shape[1]
    width = wide.shape[1]
    group = math.gcd(fine_rows, 4)
    slabs_g = p_slabs.reshape(fine_rows // group, group, block, touched * block)
    kinds_g = p_kinds.reshape(fine_rows // group, group, touched)
    wide_g = wide.reshape(fine_rows // group, group, block, width)

    def step(total, pieces):
        slab_part, kind_part, wide_part = pieces
        folded = jnp.einsum(
            "ire,irq->ieq",
            slab_part.astype(jnp.float32),
            wide_part,
            precision=lax.Precision.HIGHEST,
        )
        onehot = (kind_part[:, :, None] == lax.iota(jnp.int32, coarse)[None, None, :]).astype(
            jnp.float32
        )
        placed = jnp.einsum(
            "imn,imeq->neq",
            onehot,
            folded.reshape(group, touched, block, width),
            precision=lax.Precision.HIGHEST,
        )
        return (total + placed.reshape(coarse * block, width), None)

    start_total = jnp.zeros((coarse * block, width), jnp.float32)
    total, unused = lax.scan(step, start_total, (slabs_g, kinds_g, wide_g))
    return total


def shards(a_vals, a_cols, p_vals, p_cols):
    n_row = lax.axis_size("row")
    n_col = lax.axis_size("col")
    ratio = n_row // n_col
    block = a_vals.shape[2]
    per_row = a_cols.shape[2]
    touched = p_cols.shape[1]
    fine_rows = a_vals.shape[0]
    col_index = lax.axis_index("col")
    vals_r, ids_r = (
        lax.all_gather(p_vals, "col", axis=0, tiled=True),
        lax.all_gather(p_cols, "col", axis=0, tiled=True),
    )
    got_vals = []
    got_ids = []
    for offset in range(ratio):
        one_vals, one_ids = (
            from_root(vals_r, "row", ratio * col_index + offset),
            from_root(ids_r, "row", ratio * col_index + offset),
        )
        got_vals.append(one_vals)
        got_ids.append(one_ids)
    vals_c = jnp.concatenate(got_vals, axis=0)
    ids_c = jnp.concatenate(got_ids, axis=0)
    group = math.gcd(fine_rows, 4)
    tiles_a = a_vals[:, 0].reshape(fine_rows // group, group, block, per_row, block)
    where_a = a_cols[:, 0].reshape(fine_rows // group, group, per_row)

    def one_group(pair):
        tiles_part, where = pair
        flat_where = where.reshape(-1)
        picked = vals_c[flat_where].reshape(group, per_row, block, touched * block)
        kinds = ids_c[flat_where].reshape(group, per_row * touched)
        product = jnp.einsum(
            "irkf,ikfe->irke", tiles_part, picked, preferred_element_type=jnp.float32
        )
        product = product.reshape(group, block, per_row * touched, block)
        onehot = (kinds[:, :, None] == lax.iota(jnp.int32, n_row)[None, None, :]).astype(
            jnp.float32
        )
        placed = jnp.einsum("irsd,isn->irnd", product, onehot, precision=lax.Precision.HIGHEST)
        return placed.reshape(group * block, n_row * block)

    partial_w = lax.map(one_group, (tiles_a, where_a)).reshape(fine_rows * block, n_row * block)
    rows_out = n_row * block // n_row
    cols_out = n_row * block // n_col
    total = contract_rows(vals_r, ids_r, partial_w, n_row)
    total = total.reshape(n_row, rows_out, n_col, cols_out)
    total = jnp.transpose(total, (0, 2, 1, 3)).reshape(n_row * n_col * rows_out, cols_out)
    return lax.psum_scatter(total, ("row", "col"), scatter_dimension=0, tiled=True)


def solution(mesh):
    in_specs = (
        P("row", "col", None, None),
        P("row", "col", None),
        P(("row", "col"), None, None),
        P(("row", "col"), None),
    )
    out_specs = P("row", "col")
    return jax.shard_map(shards, mesh=mesh, in_specs=in_specs, out_specs=out_specs, check_vma=False)
```

profile of v0, /device:TPU:0, one launch (start us, length us, event | category | flops | bytes accessed | tf_op | source)
XLA Modules:
  0.0 1219.6 jit_solution(4784218886099866676)
XLA Ops:
  7.3 45.0 %all-gather.3.cloned.1.call-done = bf16[32,64,256]{2,1,0:T(8,128)(2,1)} async-done(((bf16[4,64,256]{2,1,0:T(8,128)(2,1)}), bf16[32,64,256]{2,1,0:T(8,128)(2,1)}) %all-gather.3.cloned.1.call-update) | async-done | bytes 1048592 | tf_op jit(solution)/shard_map/all_gather | solution.py:57
  55.1 24.8 %all-gather = s32[8,4,4]{2,1,0:T(4,128)S(1)} all-gather(s32[1,4,4]{2,1,0:T(4,128)S(1)} %bitcast.92), channel_id=1, replica_groups=mesh['row'=16,'col'=8] {'col'}, dimensions={0}, use_global_device_ids=true | all-gather | bytes 576 | tf_op jit(solution)/shard_map/all_gather | solution.py:58
  80.0 13.7 %all-reduce = (s32[32,4]{0,1:T(4,128)S(1)}, s32[32,4]{0,1:T(4,128)S(1)}) all-reduce(s32[32,4]{0,1:T(4,128)S(1)} %copy.32, s32[32,4]{0,1:T(4,128)S(1)} %copy.31), channel_id=1, replica_groups=mesh['row'=16,'col'=8] {'row'}, use_global_device_ids=true, to_apply=%region_3.4 | all-reduce | flops 256 | bytes 2048 | tf_op jit(solution)/shard_map/psum | solution.py:10
  93.9 11.6 reshape_squeeze.7
  105.6 94.5 %all-reduce.4.cloned.1.call-done = (bf16[32,64,256]{2,1,0:T(8,128)(2,1)}, bf16[32,64,256]{2,1,0:T(8,128)(2,1)}) async-done(((bf16[32,64,256]{2,1,0:T(8,128)(2,1)}, bf16[32,64,256]{2,1,0:T(8,128)(2,1)}), (bf16[32,64,256]{2,1,0:T(8,128)(2,1)}, bf16[32,64,256]{2,1,0:T(8,128)(2,1)})) %all-reduce.4.cloned.1.call-update) | async-done | bytes 2097168 | tf_op jit(solution)/shard_map/psum | solution.py:10
  203.2 186.4 %while.21 = (s32[]{:T(128)}, f32[8,256,1024]{2,1,0:T(8,128)}, s32[8,4,16]{2,1,0:T(4,128)S(1)}, s32[64,4]{1,0:T(8,128)S(1)}, bf16[64,64,256]{2,1,0:T(8,128)(2,1)}, /*index=5*/bf16[8,4,64,16,64]{4,3,2,1,0:T(8,128)(2,1)}, s32[]{:T(128)}) while((s32[]{:T(128)}, f32[8,256,1024]{2,1,0:T(8,128)}, s32[8,4,16]{2,1,0:T(4,128)S(1)}, ...), condition=%wide.region_5.6_spmd, body=%wide.region_4.5_spmd.sunk | while | flops 335549632 | bytes 38285140 | solution.py:90
  212.0 7.0 reshape.107
  219.7 5.2 convolution_bitcast_fusion.5
  235.4 7.0 reshape.107
  243.0 5.2 convolution_bitcast_fusion.5
  258.6 7.0 reshape.107
  266.3 5.2 convolution_bitcast_fusion.5
  281.9 7.0 reshape.107
  289.6 5.1 convolution_bitcast_fusion.5
  305.2 7.0 reshape.107
  312.9 5.2 convolution_bitcast_fusion.5
  328.6 7.0 reshape.107
  336.2 5.2 convolution_bitcast_fusion.5
  351.8 7.0 reshape.107
  359.5 5.2 convolution_bitcast_fusion.5
  375.1 7.0 reshape.107
  382.8 5.2 convolution_bitcast_fusion.5
  389.5 165.1 %while.22 = (s32[]{:T(128)}, f32[1024,1024]{1,0:T(8,128)}, s32[8,4,4]{2,1,0:T(4,128)S(1)}, bf16[8,4,64,256]{3,2,1,0:T(8,128)(2,1)}, f32[8,4,64,1024]{3,2,1,0:T(8,128)}, /*index=5*/s32[]{:T(128)}, s32[]{:T(128)}) while((s32[]{:T(128)}, f32[1024,1024]{1,0:T(8,128)}, s32[8,4,4]{2,1,0:T(4,128)S(1)}, bf16[8,4,64,256]{3,2,1,0:T(8,128)(2,1)}, ...), condition=%wide.region_7.8_spmd.clone, body=%wide.region_6.7_spmd.clone.sunk | while | flops 1008730368 | bytes 34735384 | solution.py:43
  392.7 6.4 fusion.39
  399.1 4.4 copy.48
  403.5 5.6 bitcast_add_fusion.2
  412.3 6.4 fusion.39
  418.6 4.4 copy.48
  423.0 6.9 bitcast_add_fusion.2
  433.1 6.4 fusion.39
  439.4 4.4 copy.48
  443.8 6.9 bitcast_add_fusion.2
  453.9 6.4 fusion.39
  460.2 4.4 copy.48
  464.6 6.9 bitcast_add_fusion.2
  474.7 6.4 fusion.39
  481.0 4.4 copy.48
  485.4 6.9 bitcast_add_fusion.2
  495.5 6.4 fusion.39
  501.8 4.4 copy.48
  506.2 6.9 bitcast_add_fusion.2
  516.3 6.4 fusion.39
  522.6 4.4 copy.48
  527.0 6.9 bitcast_add_fusion.2
  537.1 6.4 fusion.39
  543.4 4.4 copy.48
  547.8 6.9 bitcast_add_fusion.2
  560.6 652.5 %reduce-scatter.2.cloned.1.call-done = f32[64,128]{1,0:T(8,128)} async-done(((f32[8192,128]{1,0:T(8,128)}), f32[64,128]{1,0:T(8,128)}) %reduce-scatter.2.cloned.1.call-update) | async-done | bytes 32784 | tf_op jit(solution)/shard_map/reduce_scatter | solution.py:96
  (134 shorter events, 127.5 us)
Async XLA Ops:
  6.5 48.5 %copy-start.1 = (s32[4,4]{1,0:T(4,128)S(1)}, s32[4,4]{1,0:T(4,128)}, u32[]{:S(2)}) copy-start(s32[4,4]{1,0:T(4,128)} %param.11) | copy-start | bytes 196
  6.5 45.8 %all-gather.3.cloned.1.call-start = ((), (), s32[]{:S(2)}) async-start(), calls=%async_computation.1 | async-start | bytes 1179648 | tf_op jit(solution)/shard_map/all_gather | solution.py:57
  7.3 192.9 %all-reduce.4.cloned.1.call-start = ((), (), s32[]{:S(2)}) async-start(), calls=%async_computation.3 | async-start | bytes 4194304 | tf_op jit(solution)/shard_map/psum | solution.py:10
  55.0 1158.1 %reduce-scatter.2.cloned.1.call-start = ((), (), s32[]{:S(2)}) async-start(), calls=%async_computation.2 | async-start | bytes 4227072 | tf_op jit(solution)/shard_map/reduce_scatter | solution.py:96
  93.9 11.6 copy-start
Sparse Core Ops, SparseCore 0:
  9.0 43.3 all-gather.2
  55.1 144.9 all-reduce.3
  560.7 652.3 reduce-scatter.1
where the time goes:
time: 1220 us
  waiting for transfers between devices  793 us (65%)
  local copies, waits for them, and re-layouts  192 us (16%)
  matrix products  123 us (10%)
  other arithmetic  59.6 us (5%)
  blocking collectives  38.5 us (3%)
  between operations  13.2 us (1%)
    reduce_scatter x1, waiting for transfers between devices, shards(): lax.psum_scatter(total, ('row', 'col'), scatter_dimension=0, tiled=True)  653 us
    psum x1, waiting for transfers between devices, from_root(): return lax.psum(kept, axis)  94.5 us
    reshape x8, local copies, waits for them, and re-layouts, one_group(): product = product.reshape(group, block, per_row * touched, block)  55.7 us
    add x8, other arithmetic, step(): return (total + placed.reshape(coarse * block, width), None)  53.6 us
    dot_general x8, matrix products, step(): jnp.einsum('imn,imeq->neq', onehot, folded.reshape(group, touched, block,...  50.8 us
    all_gather x1, waiting for transfers between devices, shards(): lax.all_gather(p_vals, 'col', axis=0, tiled=True)  45 us
    dot_general x8, matrix products, one_group(): jnp.einsum('irsd,isn->irnd', product, onehot, precision=lax.Precision.HIG...  41.2 us
    dot_general x8, local copies, waits for them, and re-layouts, step(): jnp.einsum('imn,imeq->neq', onehot, folded.reshape(group, touched, block,...  35 us
  transfers between devices with their start and end apart: 3, of which 3 were waited for; matrix products, arithmetic and copies ran while one was open for 1% of the time, Pallas kernels for 0%

commit v1 on v0

--- a/solution.py
+++ b/solution.py
@@ -3,6 +3,13 @@
 import jax.numpy as jnp
 from jax import lax
 from jax.sharding import PartitionSpec as P
+
+
+def swapped_in(shard, name, dim):
+    size = lax.axis_size(name)
+    blocks = jnp.stack([shard for _ in range(size)])
+    blocks = lax.all_to_all(blocks, name, split_axis=0, concat_axis=0)
+    return jnp.concatenate(blocks, axis=dim)
 
 
 def from_root(value, axis, source):
@@ -54,7 +61,7 @@
     fine_rows = a_vals.shape[0]
     col_index = lax.axis_index("col")
     vals_r, ids_r = (
-        lax.all_gather(p_vals, "col", axis=0, tiled=True),
+        swapped_in(p_vals, "col", 0),
         lax.all_gather(p_cols, "col", axis=0, tiled=True),
     )
     got_vals = []

time: 1220 us -> 1200 us (0.984)
  waiting for transfers between devices: 793 us -> 761 us
    all_gather x1 -> x0, waiting for transfers between devices: 45 us -> none  [shards(): lax.all_gather(p_vals, 'col', axis=0, tiled=True)]
    all_to_all x0 -> x1, waiting for transfers between devices: none -> 15.6 us  [swapped_in(): blocks = lax.all_to_all(blocks, name, split_axis=0, concat_axis=0)]
where the time goes in v1:
time: 1200 us
  waiting for transfers between devices  761 us (63%)
  local copies, waits for them, and re-layouts  194 us (16%)
  matrix products  123 us (10%)
  other arithmetic  58.5 us (5%)
  blocking collectives  38.6 us (3%)
  between operations  13.5 us (1%)
    reduce_scatter x1, waiting for transfers between devices, shards(): lax.psum_scatter(total, ('row', 'col'), scatter_dimension=0, tiled=True)  651 us
    psum x1, waiting for transfers between devices, from_root(): return lax.psum(kept, axis)  94.5 us
    reshape x8, local copies, waits for them, and re-layouts, one_group(): product = product.reshape(group, block, per_row * touched, block)  55.7 us
    add x8, other arithmetic, step(): return (total + placed.reshape(coarse * block, width), None)  53.6 us
    dot_general x8, matrix products, step(): jnp.einsum('imn,imeq->neq', onehot, folded.reshape(group, touched, block,...  50.8 us
    dot_general x8, matrix products, one_group(): jnp.einsum('irsd,isn->irnd', product, onehot, precision=lax.Precision.HIG...  41.2 us
    dot_general x8, local copies, waits for them, and re-layouts, step(): jnp.einsum('imn,imeq->neq', onehot, folded.reshape(group, touched, block,...  35 us
    transpose x8, local copies, waits for them, and re-layouts, one_group(): jnp.einsum('irkf,ikfe->irke', tiles_part, picked, preferred_element_type=...  34.8 us
  transfers between devices with their start and end apart: 3, of which 3 were waited for; matrix products, arithmetic and copies ran while one was open for 1% of the time, Pallas kernels for 0%

profile of v1, /device:TPU:0, one launch (start us, length us, event | category | flops | bytes accessed | tf_op | source)
XLA Modules:
  0.0 1195.7 jit_solution(2940824726113619410)
XLA Ops:
  8.5 6.4 all-to-all-start
  15.0 15.6 %all-to-all-done = bf16[8,4,64,256]{3,2,1,0:T(8,128)(2,1)S(1)} async-done(((bf16[8,4,64,256]{3,2,1,0:T(8,128)(2,1)}), bf16[8,4,64,256]{3,2,1,0:T(8,128)(2,1)S(1)}, u32[]{:S(2)}, u32[]{:S(2)}) %all-to-all-start) | async-done | bytes 1048608 | tf_op jit(solution)/shard_map/all_to_all | solution.py:11
  32.3 24.9 %all-gather = s32[8,4,4]{2,1,0:T(4,128)S(1)} all-gather(s32[1,4,4]{2,1,0:T(4,128)S(1)} %bitcast.94), channel_id=1, replica_groups=mesh['row'=16,'col'=8] {'col'}, dimensions={0}, use_global_device_ids=true | all-gather | bytes 576 | tf_op jit(solution)/shard_map/all_gather | solution.py:65
  57.4 13.7 %all-reduce = (s32[32,4]{0,1:T(4,128)S(1)}, s32[32,4]{0,1:T(4,128)S(1)}) all-reduce(s32[32,4]{0,1:T(4,128)S(1)} %copy.32, s32[32,4]{0,1:T(4,128)S(1)} %copy.31), channel_id=1, replica_groups=mesh['row'=16,'col'=8] {'row'}, use_global_device_ids=true, to_apply=%region_3.4 | all-reduce | flops 256 | bytes 2048 | tf_op jit(solution)/shard_map/psum | solution.py:17
  71.2 11.6 reshape_squeeze.7
  83.0 94.5 %all-reduce.4.cloned.1.call-done = (bf16[32,64,256]{2,1,0:T(8,128)(2,1)}, bf16[32,64,256]{2,1,0:T(8,128)(2,1)}) async-done(((bf16[32,64,256]{2,1,0:T(8,128)(2,1)}, bf16[32,64,256]{2,1,0:T(8,128)(2,1)}), (bf16[32,64,256]{2,1,0:T(8,128)(2,1)}, bf16[32,64,256]{2,1,0:T(8,128)(2,1)})) %all-reduce.4.cloned.1.call-update) | async-done | bytes 2097168 | tf_op jit(solution)/shard_map/psum | solution.py:17
  180.5 186.3 %while.21 = (s32[]{:T(128)}, f32[8,256,1024]{2,1,0:T(8,128)}, s32[8,4,16]{2,1,0:T(4,128)S(1)}, s32[64,4]{1,0:T(8,128)S(1)}, bf16[64,64,256]{2,1,0:T(8,128)(2,1)}, /*index=5*/bf16[8,4,64,16,64]{4,3,2,1,0:T(8,128)(2,1)}, s32[]{:T(128)}) while((s32[]{:T(128)}, f32[8,256,1024]{2,1,0:T(8,128)}, s32[8,4,16]{2,1,0:T(4,128)S(1)}, ...), condition=%wide.region_5.6_spmd, body=%wide.region_4.5_spmd.sunk | while | flops 335549632 | bytes 38285140 | solution.py:97
  189.4 7.0 reshape.112
  197.0 5.2 convolution_bitcast_fusion.5
  212.7 7.0 reshape.112
  220.4 5.1 convolution_bitcast_fusion.5
  236.0 7.0 reshape.112
  243.6 5.1 convolution_bitcast_fusion.5
  259.2 7.0 reshape.112
  266.9 5.1 convolution_bitcast_fusion.5
  282.6 7.0 reshape.112
  290.2 5.2 convolution_bitcast_fusion.5
  305.9 7.0 reshape.112
  313.5 5.2 convolution_bitcast_fusion.5
  329.2 7.0 reshape.112
  336.8 5.1 convolution_bitcast_fusion.5
  352.4 7.0 reshape.112
  360.1 5.2 convolution_bitcast_fusion.5
  366.9 165.1 %while.22 = (s32[]{:T(128)}, f32[1024,1024]{1,0:T(8,128)}, s32[8,4,4]{2,1,0:T(4,128)S(1)}, bf16[8,4,64,256]{3,2,1,0:T(8,128)(2,1)}, f32[8,4,64,1024]{3,2,1,0:T(8,128)}, /*index=5*/s32[]{:T(128)}, s32[]{:T(128)}) while((s32[]{:T(128)}, f32[1024,1024]{1,0:T(8,128)}, s32[8,4,4]{2,1,0:T(4,128)S(1)}, bf16[8,4,64,256]{3,2,1,0:T(8,128)(2,1)}, ...), condition=%wide.region_7.8_spmd.clone, body=%wide.region_6.7_spmd.clone.sunk | while | flops 1008730368 | bytes 34735384 | solution.py:50
  370.1 6.4 fusion.39
  376.4 4.4 copy.48
  380.8 5.6 bitcast_add_fusion.2
  389.6 6.4 fusion.39
  396.0 4.4 copy.48
  400.3 6.9 bitcast_add_fusion.2
  410.4 6.4 fusion.39
  416.8 4.4 copy.48
  421.1 6.9 bitcast_add_fusion.2
  431.2 6.4 fusion.39
  437.6 4.4 copy.48
  441.9 6.9 bitcast_add_fusion.2
  452.0 6.4 fusion.39
  458.4 4.4 copy.48
  462.7 6.9 bitcast_add_fusion.2
  472.8 6.4 fusion.39
  479.2 4.4 copy.48
  483.5 6.9 bitcast_add_fusion.2
  493.6 6.4 fusion.39
  504.3 6.9 bitcast_add_fusion.2
  514.4 6.4 fusion.39
  520.8 4.4 copy.48
  525.1 6.9 bitcast_add_fusion.2
  537.9 650.9 %reduce-scatter.2.cloned.1.call-done = f32[64,128]{1,0:T(8,128)} async-done(((f32[8192,128]{1,0:T(8,128)}), f32[64,128]{1,0:T(8,128)}) %reduce-scatter.2.cloned.1.call-update) | async-done | bytes 32784 | tf_op jit(solution)/shard_map/reduce_scatter | solution.py:103
  (136 shorter events, 132.0 us)
Async XLA Ops:
  6.5 25.8 %copy-start.2 = (s32[4,4]{1,0:T(4,128)S(1)}, s32[4,4]{1,0:T(4,128)}, u32[]{:S(2)}) copy-start(s32[4,4]{1,0:T(4,128)} %param.11) | copy-start | bytes 196
  8.5 22.1 %all-to-all-start = ((bf16[8,4,64,256]{3,2,1,0:T(8,128)(2,1)}), bf16[8,4,64,256]{3,2,1,0:T(8,128)(2,1)S(1)}, u32[]{:S(2)}, u32[]{:S(2)}) async-start(bf16[8,4,64,256]{3,2,1,0:T(8,128)(2,1)} %stack.2), calls=%async_computation | async-start | bytes 2097152 | tf_op jit(solution)/shard_map/all_to_all | solution.py:11
  15.0 162.5 %all-reduce.4.cloned.1.call-start = ((), (), s32[]{:S(2)}) async-start(), calls=%async_computation.3 | async-start | bytes 4194304 | tf_op jit(solution)/shard_map/psum | solution.py:17
  30.7 52.2 %copy-start = (bf16[8,4,64,256]{3,2,1,0:T(8,128)(2,1)}, bf16[8,4,64,256]{3,2,1,0:T(8,128)(2,1)S(1)}, u32[]{:S(2)}) copy-start(bf16[8,4,64,256]{3,2,1,0:T(8,128)(2,1)S(1)} %all-to-all-done) | copy-start | bytes 3145732
  32.2 1156.6 %reduce-scatter.2.cloned.1.call-start = ((), (), s32[]{:S(2)}) async-start(), calls=%async_computation.2 | async-start | bytes 4227072 | tf_op jit(solution)/shard_map/reduce_scatter | solution.py:103
  71.2 11.6 copy-start.1
Sparse Core Ops, SparseCore 0:
  32.4 145.0 all-reduce.3
  538.0 650.7 reduce-scatter.1
